TPU v7x, 32 devices: a whole 2x2x4 slice. The times are simulated.
32 devices in a mesh: seq: 4 (over y, x), fsdp: 8 (over z, core).
Axes of the slice: x: 2, y: 2, z: 4, core: 2. Of those that a mesh axis runs over, the one named last changes fastest.
Arguments:
- tokens: bfloat16 [8, 1152, 2048], P('fsdp', 'seq'), may hold values from -6 to 6
- doc_lengths: int32 [8, 4], P('fsdp'), may hold values from 1 to 1024, as said below
- positions: int32 [8, 1152], P('fsdp'), may hold values from 0 to 2174, as said below
- cotangent: bfloat16 [8, 1152, 2048], P('fsdp', 'seq'), may hold values from -6 to 6
- w_query: bfloat16 [2048, 2048], P('fsdp'), may hold values from -0.125 to 0.125
- key_matrix: bfloat16 [2048, 1024], P('fsdp'), may hold values from -0.125 to 0.125
- value_matrix: bfloat16 [2048, 1024], P('fsdp'), may hold values from -0.125 to 0.125
- w_attn_gate: bfloat16 [2048, 2048], P('fsdp'), may hold values from -0.125 to 0.125
- w_out: bfloat16 [2048, 2048], P('fsdp'), may hold values from -1.5 to 1.5
- w_gate: bfloat16 [2048, 6144], P('fsdp'), may hold values from -0.125 to 0.125
- w_up: bfloat16 [2048, 6144], P('fsdp'), may hold values from -0.125 to 0.125
- w_down: bfloat16 [6144, 2048], P('fsdp'), may hold values from -0.078125 to 0.078125
- gain_attn: bfloat16 [2048], P('fsdp'), may hold values from 0.25 to 1.75
- gain_mlp: bfloat16 [2048], P('fsdp'), may hold values from 0.25 to 1.75
Outputs:
- block_output: bfloat16 [8, 1152, 2048], P('fsdp', 'seq')
- grad_tokens: bfloat16 [8, 1152, 2048], P('fsdp', 'seq')
- grad_w_query: float32 [2048, 2048], P('fsdp')
- grad_w_key: float32 [2048, 1024], P('fsdp')
- grad_w_value: float32 [2048, 1024], P('fsdp')
- grad_w_attn_gate: float32 [2048, 2048], P('fsdp')
- grad_w_out: float32 [2048, 2048], P('fsdp')
- grad_w_gate: float32 [2048, 6144], P('fsdp')
- grad_w_up: float32 [2048, 6144], P('fsdp')
- grad_w_down: float32 [6144, 2048], P('fsdp')
- grad_gain_attn: float32 [2048], P('fsdp')
- grad_gain_mlp: float32 [2048], P('fsdp')
Inputs may be any that keep to these rules, and one draw needn't show every extreme that they name: `doc_lengths`: each pack's 4 document lengths sum to 1152, and the largest is exactly 1024. `positions`: a token's position is its index within its document plus an offset shared by the whole document, below 1152; the longest document's offset is the largest.
All inputs are finite; a program needn't handle non-finite values.
Results may differ from a plain program's by a relative error of at most 0.02.
Values may be sent and summed in bfloat16 or wider, within the bound.
No kernel may reach another device: no remote copies, remote signals or barrier semaphores. Data moves between devices by JAX's collectives and lax.ppermute only.
A program may use at most 512 MiB of HBM per device.

v0:
```python
import jax
import jax.numpy as jnp
from jax import lax
from jax.sharding import PartitionSpec as P

QUERY_HEADS = 16
KEY_VALUE_HEADS = 8
HEAD_DIM = 128
QB = 576
epsilon = 1e-06
rope_base = 1000000.0
masked_value = -1e30


def dot_plain(left_mat, right_mat):
    return jnp.dot(left_mat, right_mat, preferred_element_type=jnp.float32)


def dot_rows(left_mat, right_mat):
    return lax.dot_general(
        left_mat, right_mat, (((0,), (0,)), ((), ())), preferred_element_type=jnp.float32
    )


def dot_back(left_mat, right_mat):
    return lax.dot_general(
        left_mat, right_mat, (((1,), (1,)), ((), ())), preferred_element_type=jnp.float32
    )


def rms_parts(values):
    inv_scale = lax.rsqrt(jnp.mean(values * values, axis=-1, keepdims=True) + epsilon)
    return (values * inv_scale, inv_scale)


def rms_back(grad_normed_out, normed, inv_scale, gain):
    grad_gain = jnp.sum(grad_normed_out * normed, axis=0)
    grad_normed = grad_normed_out * gain
    grad_input = inv_scale * (
        grad_normed - normed * jnp.mean(grad_normed * normed, axis=-1, keepdims=True)
    )
    return (grad_input, grad_gain)


def angles_of(positions):
    half_dim = HEAD_DIM // 2
    frequency = rope_base ** (-(2.0 * jnp.arange(half_dim, dtype=jnp.float32)) / HEAD_DIM)
    return positions.astype(jnp.float32)[:, None] * frequency[None, :]


def apply_rotation(values, rotary_angles):
    half_dim = values.shape[-1] // 2
    cosine = jnp.cos(rotary_angles)[:, None, :]
    sine_part = jnp.sin(rotary_angles)[:, None, :]
    leading = values[..., :half_dim]
    trailing = values[..., half_dim:]
    return jnp.concatenate(
        [leading * cosine - trailing * sine_part, trailing * cosine + leading * sine_part], axis=-1
    )


def shards(
    tokens,
    doc_lengths,
    positions,
    cotangent,
    w_query,
    key_matrix,
    value_matrix,
    w_attn_gate,
    w_out,
    w_gate,
    w_up,
    w_down,
    gain_attn,
    gain_mlp,
):
    inputs = tokens[0].astype(jnp.float32)
    local_rows = inputs.shape[0]
    grad_out = cotangent[0]
    normed_attn, scale_attn = rms_parts(inputs)
    full_query, full_key, full_value, full_attn_gate, full_out, full_gain_attn, full_gain_mlp = (
        lax.all_gather(w_query, "fsdp", axis=0, tiled=True),
        lax.all_gather(key_matrix, "fsdp", axis=0, tiled=True),
        lax.all_gather(value_matrix, "fsdp", axis=0, tiled=True),
        lax.all_gather(w_attn_gate, "fsdp", axis=0, tiled=True),
        lax.all_gather(w_out, "fsdp", axis=0, tiled=True),
        lax.all_gather(gain_attn, "fsdp", axis=0, tiled=True),
        lax.all_gather(gain_mlp, "fsdp", axis=0, tiled=True),
    )
    gain_attn_f = full_gain_attn.astype(jnp.float32)
    gain_mlp_f = full_gain_mlp.astype(jnp.float32)
    hidden_attention = (normed_attn * gain_attn_f).astype(jnp.bfloat16)
    query_rows = (
        dot_plain(hidden_attention, full_query)
        .astype(jnp.bfloat16)
        .reshape(local_rows, -1, HEAD_DIM)
    )
    keys_tok = (
        dot_plain(hidden_attention, full_key).astype(jnp.bfloat16).reshape(local_rows, -1, HEAD_DIM)
    )
    values_tok = (
        dot_plain(hidden_attention, full_value)
        .astype(jnp.bfloat16)
        .reshape(local_rows, -1, HEAD_DIM)
    )
    gates_tok = (
        dot_plain(hidden_attention, full_attn_gate)
        .astype(jnp.bfloat16)
        .reshape(local_rows, -1, HEAD_DIM)
    )
    q_heads, k_heads, v_heads, g_heads = (
        lax.all_to_all(query_rows, "seq", split_axis=1, concat_axis=0, tiled=True),
        lax.all_to_all(keys_tok, "seq", split_axis=1, concat_axis=0, tiled=True),
        lax.all_to_all(values_tok, "seq", split_axis=1, concat_axis=0, tiled=True),
        lax.all_to_all(gates_tok, "seq", split_axis=1, concat_axis=0, tiled=True),
    )
    pack_len = q_heads.shape[0]
    local_q = q_heads.shape[1]
    local_kv = k_heads.shape[1]
    query_group_width = QUERY_HEADS // KEY_VALUE_HEADS
    token_index = jnp.arange(pack_len, dtype=jnp.int32)
    doc_ends = jnp.cumsum(doc_lengths[0])
    segment = jnp.sum((token_index[:, None] >= doc_ends[None, :]).astype(jnp.int32), axis=1)
    rotary_angles = angles_of(positions[0])
    q_rot = (
        apply_rotation(q_heads.astype(jnp.float32), rotary_angles)
        .astype(jnp.bfloat16)
        .reshape(pack_len, local_kv, query_group_width, HEAD_DIM)
    )
    k_rot = apply_rotation(k_heads.astype(jnp.float32), rotary_angles).astype(jnp.bfloat16)
    scale_factor = HEAD_DIM ** (-0.5)
    block_starts = jnp.arange(pack_len // QB, dtype=jnp.int32) * QB

    def block_scores(block_start):
        q_block = lax.dynamic_slice_in_dim(q_rot, block_start, QB, 0)
        raw_scores = (
            jnp.einsum("qhgd,khd->hgqk", q_block, k_rot, preferred_element_type=jnp.float32)
            * scale_factor
        )
        row_ids = block_start + jnp.arange(QB, dtype=jnp.int32)
        row_segment = lax.dynamic_slice_in_dim(segment, block_start, QB, 0)
        allowed = (row_segment[:, None] == segment[None, :]) & (
            row_ids[:, None] >= token_index[None, :]
        )
        return (q_block, jnp.where(allowed[None, None], raw_scores, masked_value))

    def attend_block(block_start):
        q_block, scores = block_scores(block_start)
        row_max = jnp.max(scores, axis=-1, keepdims=True)
        exp_scores = jnp.exp(scores - row_max)
        row_total = jnp.sum(exp_scores, axis=-1, keepdims=True)
        attn_probs = exp_scores / row_total
        log_total = (row_max + jnp.log(row_total))[..., 0]
        mixed_block = jnp.einsum(
            "hgqk,khd->qhgd",
            attn_probs.astype(jnp.bfloat16),
            v_heads,
            preferred_element_type=jnp.float32,
        )
        return (mixed_block, log_total)

    mixed_blocks, lse_blocks = lax.map(attend_block, block_starts)
    mixed_heads = mixed_blocks.reshape(pack_len, local_q, HEAD_DIM)
    gate_sig = jax.nn.sigmoid(g_heads.astype(jnp.float32))
    gated_heads = (mixed_heads * gate_sig).astype(jnp.bfloat16)
    gated_tok = lax.all_to_all(gated_heads, "seq", split_axis=0, concat_axis=1, tiled=True).reshape(
        local_rows, -1
    )
    residual = inputs + dot_plain(gated_tok, full_out)
    normed_mlp, scale_mlp = rms_parts(residual)
    h_mlp = (normed_mlp * gain_mlp_f).astype(jnp.bfloat16)
    full_gate, full_up, full_down = (
        lax.all_gather(w_gate, "fsdp", axis=0, tiled=True),
        lax.all_gather(w_up, "fsdp", axis=0, tiled=True),
        lax.all_gather(w_down, "fsdp", axis=0, tiled=True),
    )
    gate_pre = dot_plain(h_mlp, full_gate)
    up_pre = dot_plain(h_mlp, full_up)
    sig_gate = jax.nn.sigmoid(gate_pre)
    silu_gate = gate_pre * sig_gate
    hidden = (silu_gate * up_pre).astype(jnp.bfloat16)
    output = residual + dot_plain(hidden, full_down)
    grad_hidden = dot_back(grad_out, full_down)
    grad_gate_pre = (grad_hidden * up_pre * sig_gate * (1.0 + gate_pre * (1.0 - sig_gate))).astype(
        jnp.bfloat16
    )
    grad_up_pre = (grad_hidden * silu_gate).astype(jnp.bfloat16)
    grad_gate_up = jnp.concatenate([grad_gate_pre, grad_up_pre], axis=1)
    gate_up_part = lax.psum_scatter(
        dot_rows(h_mlp, grad_gate_up).astype(jnp.bfloat16), "fsdp", scatter_dimension=0, tiled=True
    )
    down_part = lax.psum_scatter(
        dot_rows(hidden, grad_out).astype(jnp.bfloat16), "fsdp", scatter_dimension=0, tiled=True
    )
    grad_h_mlp = dot_back(grad_gate_pre, full_gate) + dot_back(grad_up_pre, full_up)
    grad_res_mlp, grad_gain_mlp = rms_back(grad_h_mlp, normed_mlp, scale_mlp, gain_mlp_f)
    grad_resid = grad_out.astype(jnp.float32) + grad_res_mlp
    grad_attn_out = grad_resid.astype(jnp.bfloat16)
    grad_w_out = dot_rows(gated_tok, grad_attn_out)
    grad_gated = (
        dot_back(grad_attn_out, full_out).astype(jnp.bfloat16).reshape(local_rows, -1, HEAD_DIM)
    )
    grad_gated_heads = lax.all_to_all(
        grad_gated, "seq", split_axis=1, concat_axis=0, tiled=True
    ).astype(jnp.float32)
    grad_mixed = (
        (grad_gated_heads * gate_sig)
        .astype(jnp.bfloat16)
        .reshape(pack_len, local_kv, query_group_width, HEAD_DIM)
    )
    grad_gate_logits = (grad_gated_heads * mixed_heads * gate_sig * (1.0 - gate_sig)).astype(
        jnp.bfloat16
    )

    def back_block(state_in, block_items):
        grad_keys, grad_values = state_in
        block_start, log_total = block_items
        q_block, scores = block_scores(block_start)
        attn_probs = jnp.exp(scores - log_total[..., None])
        grad_block = lax.dynamic_slice_in_dim(grad_mixed, block_start, QB, 0)
        grad_probs = jnp.einsum(
            "qhgd,khd->hgqk", grad_block, v_heads, preferred_element_type=jnp.float32
        )
        row_delta = jnp.sum(attn_probs * grad_probs, axis=-1, keepdims=True)
        grad_scores = (attn_probs * (grad_probs - row_delta) * scale_factor).astype(jnp.bfloat16)
        grad_q_block = jnp.einsum(
            "hgqk,khd->qhgd", grad_scores, k_rot, preferred_element_type=jnp.float32
        )
        grad_keys = grad_keys + jnp.einsum(
            "hgqk,qhgd->khd", grad_scores, q_block, preferred_element_type=jnp.float32
        )
        grad_values = grad_values + jnp.einsum(
            "hgqk,qhgd->khd",
            attn_probs.astype(jnp.bfloat16),
            grad_block,
            preferred_element_type=jnp.float32,
        )
        return ((grad_keys, grad_values), grad_q_block)

    zero_keys = jnp.zeros((pack_len, local_kv, HEAD_DIM), jnp.float32)
    (grad_k_sum, grad_v_sum), grad_q_blocks = lax.scan(
        back_block, (zero_keys, zero_keys), (block_starts, lse_blocks)
    )
    grad_q = apply_rotation(
        grad_q_blocks.reshape(pack_len, local_q, HEAD_DIM), -rotary_angles
    ).astype(jnp.bfloat16)
    grad_k = apply_rotation(grad_k_sum, -rotary_angles).astype(jnp.bfloat16)
    grad_v = grad_v_sum.astype(jnp.bfloat16)
    dq_tok, dk_tok, dv_tok, dg_tok = (
        lax.all_to_all(grad_q, "seq", split_axis=0, concat_axis=1, tiled=True),
        lax.all_to_all(grad_k, "seq", split_axis=0, concat_axis=1, tiled=True),
        lax.all_to_all(grad_v, "seq", split_axis=0, concat_axis=1, tiled=True),
        lax.all_to_all(grad_gate_logits, "seq", split_axis=0, concat_axis=1, tiled=True),
    )
    dq_tok = dq_tok.reshape(local_rows, -1)
    dk_tok = dk_tok.reshape(local_rows, -1)
    dv_tok = dv_tok.reshape(local_rows, -1)
    dg_tok = dg_tok.reshape(local_rows, -1)
    grad_w_query = dot_rows(hidden_attention, dq_tok)
    grad_w_key = dot_rows(hidden_attention, dk_tok)
    grad_w_value = dot_rows(hidden_attention, dv_tok)
    grad_w_attn_gate = dot_rows(hidden_attention, dg_tok)
    grad_h_attn = (
        dot_back(dq_tok, full_query)
        + dot_back(dk_tok, full_key)
        + dot_back(dv_tok, full_value)
        + dot_back(dg_tok, full_attn_gate)
    )
    grad_res_attn, grad_gain_attn = rms_back(grad_h_attn, normed_attn, scale_attn, gain_attn_f)
    grad_tokens = (grad_resid + grad_res_attn).astype(jnp.bfloat16)[None]
    part_query, part_key, part_value, part_attn_gate, part_out, part_gain_attn, part_gain_mlp = (
        lax.psum_scatter(
            grad_w_query.astype(jnp.bfloat16), "fsdp", scatter_dimension=0, tiled=True
        ).astype(jnp.float32),
        lax.psum_scatter(
            grad_w_key.astype(jnp.bfloat16), "fsdp", scatter_dimension=0, tiled=True
        ).astype(jnp.float32),
        lax.psum_scatter(
            grad_w_value.astype(jnp.bfloat16), "fsdp", scatter_dimension=0, tiled=True
        ).astype(jnp.float32),
        lax.psum_scatter(
            grad_w_attn_gate.astype(jnp.bfloat16), "fsdp", scatter_dimension=0, tiled=True
        ).astype(jnp.float32),
        lax.psum_scatter(
            grad_w_out.astype(jnp.bfloat16), "fsdp", scatter_dimension=0, tiled=True
        ).astype(jnp.float32),
        lax.psum_scatter(
            grad_gain_attn.astype(jnp.bfloat16), "fsdp", scatter_dimension=0, tiled=True
        ).astype(jnp.float32),
        lax.psum_scatter(
            grad_gain_mlp.astype(jnp.bfloat16), "fsdp", scatter_dimension=0, tiled=True
        ).astype(jnp.float32),
    )
    (
        sum_gate_up,
        sum_down,
        sum_query,
        sum_key,
        sum_value,
        sum_attn_gate,
        sum_out,
        sum_gain_attn,
        sum_gain_mlp,
    ) = (
        lax.psum(gate_up_part, "seq").astype(jnp.float32),
        lax.psum(down_part, "seq").astype(jnp.float32),
        lax.psum(part_query.astype(jnp.bfloat16), "seq").astype(jnp.float32),
        lax.psum(part_key.astype(jnp.bfloat16), "seq").astype(jnp.float32),
        lax.psum(part_value.astype(jnp.bfloat16), "seq").astype(jnp.float32),
        lax.psum(part_attn_gate.astype(jnp.bfloat16), "seq").astype(jnp.float32),
        lax.psum(part_out.astype(jnp.bfloat16), "seq").astype(jnp.float32),
        lax.psum(part_gain_attn.astype(jnp.bfloat16), "seq").astype(jnp.float32),
        lax.psum(part_gain_mlp.astype(jnp.bfloat16), "seq").astype(jnp.float32),
    )
    split_at = sum_gate_up.shape[1] // 2
    sum_gate = sum_gate_up[:, :split_at]
    sum_up = sum_gate_up[:, split_at:]
    return (
        output.astype(jnp.bfloat16)[None],
        grad_tokens,
        sum_query,
        sum_key,
        sum_value,
        sum_attn_gate,
        sum_out,
        sum_gate,
        sum_up,
        sum_down,
        sum_gain_attn,
        sum_gain_mlp,
    )


def solution(mesh):
    in_specs = (
        P("fsdp", "seq", None),
        P("fsdp", None),
        P("fsdp", None),
        P("fsdp", "seq", None),
        P("fsdp", None),
        P("fsdp", None),
        P("fsdp", None),
        P("fsdp", None),
        P("fsdp", None),
        P("fsdp", None),
        P("fsdp", None),
        P("fsdp", None),
        P("fsdp"),
        P("fsdp"),
    )
    out_specs = (
        P("fsdp", "seq", None),
        P("fsdp", "seq", None),
        P("fsdp", None),
        P("fsdp", None),
        P("fsdp", None),
        P("fsdp", None),
        P("fsdp", None),
        P("fsdp", None),
        P("fsdp", None),
        P("fsdp", None),
        P("fsdp"),
        P("fsdp"),
    )
    return jax.shard_map(shards, mesh=mesh, in_specs=in_specs, out_specs=out_specs, check_vma=False)
```

profile of v0, /device:TPU:0, one launch (start us, length us, event | category | flops | bytes accessed | tf_op | source)
XLA Modules:
  0.0 2623.2 jit_solution(13021053463534006150)
XLA Ops:
  12.7 13.6 all-gather
  33.1 26.1 all-gather.13.cloned.1.call-done
  67.4 39.1 %all-gather.15.cloned.1.call-done = bf16[2048,1024]{1,0:T(8,128)(2,1)} async-done(((bf16[256,1024]{1,0:T(8,128)(2,1)}), bf16[2048,1024]{1,0:T(8,128)(2,1)}) %all-gather.15.cloned.1.call-update) | async-done | bytes 4194320 | tf_op jit(solution)/shard_map/all_gather | solution.py:85
  114.7 74.3 %all-gather.11.cloned.1.call-done = bf16[2048,2048]{1,0:T(8,128)(2,1)} async-done(((bf16[256,2048]{1,0:T(8,128)(2,1)}), bf16[2048,2048]{1,0:T(8,128)(2,1)}) %all-gather.11.cloned.1.call-update) | async-done | bytes 8388624 | tf_op jit(solution)/shard_map/all_gather | solution.py:83
  189.0 6.0 fusion.82
  201.8 69.2 %all-gather.17.cloned.1.call-done = bf16[2048,2048]{1,0:T(8,128)(2,1)} async-done(((bf16[256,2048]{1,0:T(8,128)(2,1)}), bf16[2048,2048]{1,0:T(8,128)(2,1)}) %all-gather.17.cloned.1.call-update) | async-done | bytes 8388624 | tf_op jit(solution)/shard_map/all_gather | solution.py:86
  271.0 6.1 fusion.83
  286.1 12.5 all-to-all-done.3
  306.2 32.7 %while.28 = (s32[]{:T(128)}, f32[2,576,2,2,128]{4,1,0,3,2:T(8,128)}, f32[2,2,2,576]{3,2,1,0:T(2,128)}, s32[2]{0:T(128)S(1)}, s32[1152]{0:T(1024)S(1)}, /*index=5...) while((s32[]{:T(128)}, ...), condition=%wide.region_6.7_spmd.clone, body=%wide.region_3.6_spmd.clone.sunk | while | flops 1392793856 | bytes 37545896 | solution.py:163
  341.0 6.8 copy.153
  351.3 9.0 all-gather.1
  368.3 5.9 multiply_reduce_fusion.2
  375.1 197.8 %all-gather.21.cloned.1.call-done = bf16[2048,6144]{1,0:T(8,128)(2,1)} async-done(((bf16[256,6144]{1,0:T(8,128)(2,1)}), bf16[2048,6144]{1,0:T(8,128)(2,1)}) %all-gather.21.cloned.1.call-update) | async-done | bytes 25165840 | tf_op jit(solution)/shard_map/all_gather | solution.py:174
  572.9 16.4 fusion.106
  589.2 203.3 %all-gather.23.cloned.1.call-done = bf16[2048,6144]{1,0:T(8,128)(2,1)} async-done(((bf16[256,6144]{1,0:T(8,128)(2,1)}), bf16[2048,6144]{1,0:T(8,128)(2,1)}) %all-gather.23.cloned.1.call-update) | async-done | bytes 25165840 | tf_op jit(solution)/shard_map/all_gather | solution.py:175
  792.6 15.2 fusion.107
  807.8 204.5 %all-gather.25.cloned.1.call-done = bf16[6144,2048]{1,0:T(8,128)(2,1)} async-done(((bf16[768,2048]{1,0:T(8,128)(2,1)}), bf16[6144,2048]{1,0:T(8,128)(2,1)}) %all-gather.25.cloned.1.call-update) | async-done | bytes 25165840 | tf_op jit(solution)/shard_map/all_gather | solution.py:176
  1012.3 20.9 multiply_convert_fusion
  1033.2 14.5 fusion.108
  1047.7 15.7 multiply_reduce_fusion
  1066.4 6.9 fusion.84
  1078.2 15.6 all-to-all-done.5
  1097.9 114.7 %while.29 = (s32[]{:T(128)}, f32[1152,2,128]{0,2,1:T(8,128)}, f32[1152,2,128]{0,2,1:T(8,128)S(1)}, f32[2,576,2,2,128]{4,1,0,3,2:T(8,128)}, s32[2]{0:T(128)S(1)},...) while((s32[]{:T(128)}, f32[1152,2,128]{0,2,1:T(8,128)}, ...), condition=%wide.region_11.12_spmd.clone, body=%wide.region_9.11_spmd.clone.sunk | while | flops 3437723136 | bytes 128183776 | solution.py:242
  1102.8 8.0 fusion.178
  1116.2 16.4 fusion.182
  1132.6 17.1 fusion.180
  1159.8 8.0 fusion.178
  1173.3 16.4 fusion.182
  1189.7 17.4 fusion.180
  1219.0 11.6 all_to_all.129
  1237.0 10.2 all_to_all.130
  1255.4 8.2 convolution_convert_fusion.2
  1273.7 15.5 all_to_all.131
  1290.5 6.9 convolution_convert_fusion.4
  1308.3 14.4 all_to_all.132
  1324.0 7.0 convolution_convert_fusion.3
  1332.2 18.7 convolution_convert_fusion.1
  1352.2 33.7 %convolution_convert_fusion = bf16[2048,12288]{1,0:T(8,128)(2,1)} fusion(bf16[288,2048]{1,0:T(8,128)(2,1)S(1)} %copy-done.27, bf16[288,6144]{1,0:T(8,128)(2,1)} %get-tuple-element.240, bf16[288,6144]{1,0:T(8,128)(2,1)} %get-tuple-element.241), kind=kOutput, calls=%fused_computation.61 | convolution fusion | flops 14534836224 | bytes 58589184 | tf_op jit(solution)/shard_map/dot_general | solution.py:20
  1386.0 38.3 %reduce-scatter.18.cloned.1.call-done = bf16[256,2048]{1,0:T(8,128)(2,1)} async-done(((bf16[2048,2048]{1,0:T(8,128)(2,1)}), bf16[256,2048]{1,0:T(8,128)(2,1)}) %reduce-scatter.18.cloned.1.call-update) | async-done | bytes 1048592 | tf_op jit(solution)/shard_map/reduce_scatter | solution.py:285
  1424.4 90.2 %reduce-scatter.10.cloned.1.call-done = bf16[256,2048]{1,0:T(8,128)(2,1)} async-done(((bf16[2048,2048]{1,0:T(8,128)(2,1)}), bf16[256,2048]{1,0:T(8,128)(2,1)}) %reduce-scatter.10.cloned.1.call-update) | async-done | bytes 1048592 | tf_op jit(solution)/shard_map/reduce_scatter | solution.py:273
  1514.5 90.3 %reduce-scatter.16.cloned.1.call-done = bf16[256,2048]{1,0:T(8,128)(2,1)} async-done(((bf16[2048,2048]{1,0:T(8,128)(2,1)}), bf16[256,2048]{1,0:T(8,128)(2,1)}) %reduce-scatter.16.cloned.1.call-update) | async-done | bytes 1048592 | tf_op jit(solution)/shard_map/reduce_scatter | solution.py:282
  1604.8 247.8 %reduce-scatter.20.cloned.1.call-done = bf16[768,2048]{1,0:T(8,128)(2,1)} async-done(((bf16[6144,2048]{1,0:T(8,128)(2,1)}), bf16[768,2048]{1,0:T(8,128)(2,1)}) %reduce-scatter.20.cloned.1.call-update) | async-done | bytes 3145744 | tf_op jit(solution)/shard_map/reduce_scatter | solution.py:193
  1852.6 483.8 %reduce-scatter.22.cloned.1.call-done = bf16[256,12288]{1,0:T(8,128)(2,1)} async-done(((bf16[2048,12288]{1,0:T(8,128)(2,1)}), bf16[256,12288]{1,0:T(8,128)(2,1)}) %reduce-scatter.22.cloned.1.call-update) | async-done | bytes 6291472
  2338.3 15.3 fusion.67
  2368.4 14.6 all-reduce.3
  2385.1 11.1 all-reduce.4
  2402.8 193.6 %all-reduce.8.cloned.1.call-done = (bf16[256,2048]{1,0:T(8,128)(2,1)}, bf16[256,1024]{1,0:T(8,128)(2,1)}, bf16[256,1024]{1,0:T(8,128)(2,1)}, bf16[256,2048]{1,0:...) async-done(((bf16[256,2048]{1,0:T(8,128)(2,1)}, bf16[256,1024]{1,0:T(8,128)(2,1)}, bf16[256,1024]{1,0:T(8,128)(2,1)}, ...) | async-done | bytes 13631504 | tf_op jit(solution)/shard_map/psum | solution.py:308
  2596.3 9.4 fusion.105
  (265 shorter events, 216.1 us)
Async XLA Ops:
  7.2 52.0 %all-gather.13.cloned.1.call-start = ((), (), s32[]{:S(2)}) async-start(), calls=%async_computation.18 | async-start | bytes 4718592 | tf_op jit(solution)/shard_map/all_gather | solution.py:84
  7.9 98.6 %all-gather.15.cloned.1.call-start = ((), (), s32[]{:S(2)}) async-start(), calls=%async_computation.19 | async-start | bytes 4718592 | tf_op jit(solution)/shard_map/all_gather | solution.py:85
  8.7 180.3 %all-gather.11.cloned.1.call-start = ((), (), s32[]{:S(2)}) async-start(), calls=%async_computation.17 | async-start | bytes 9437184 | tf_op jit(solution)/shard_map/all_gather | solution.py:83
  9.4 261.6 %all-gather.17.cloned.1.call-start = ((), (), s32[]{:S(2)}) async-start(), calls=%async_computation.20 | async-start | bytes 9437184 | tf_op jit(solution)/shard_map/all_gather | solution.py:86
  10.0 358.3 %all-gather.19.cloned.1.call-start = ((), (), s32[]{:S(2)}) async-start(), calls=%async_computation.21 | async-start | bytes 9437184 | tf_op jit(solution)/shard_map/all_gather | solution.py:87
  10.6 562.3 %all-gather.21.cloned.1.call-start = ((), (), s32[]{:S(2)}) async-start(), calls=%async_computation.22 | async-start | bytes 28311552 | tf_op jit(solution)/shard_map/all_gather | solution.py:174
  11.1 781.4 %all-gather.23.cloned.1.call-start = ((), (), s32[]{:S(2)}) async-start(), calls=%async_computation.23 | async-start | bytes 28311552 | tf_op jit(solution)/shard_map/all_gather | solution.py:175
  11.9 14.4 copy-start.48
  11.9 15.1 copy-start.45
  11.9 15.2 copy-start.5
  11.9 1000.4 %all-gather.25.cloned.1.call-start = ((), (), s32[]{:S(2)}) async-start(), calls=%async_computation.24 | async-start | bytes 28311552 | tf_op jit(solution)/shard_map/all_gather | solution.py:176
  26.3 244.7 %copy-start.40 = (f32[8,1,256]{2,1,0:T(1,128)}, f32[8,1,256]{2,1,0:T(1,128)S(1)}, u32[]{:S(2)}) copy-start(f32[8,1,256]{2,1,0:T(1,128)S(1)} %convert_element_type.307) | copy-start | bytes 24580
  27.5 161.5 %copy-start.42 = (f32[288]{0:T(512)}, f32[288]{0:T(512)S(1)}, u32[]{:S(2)}) copy-start(f32[288]{0:T(512)S(1)} %add_rsqrt_fusion.1) | copy-start | bytes 3460
  63.8 47.3 %all-to-all-start.1 = ((bf16[288,8,128]{2,0,1:T(8,128)(2,1)}), bf16[288,8,128]{2,0,1:T(8,128)(2,1)S(1)}, u32[]{:S(2)}, u32[]{:S(2)}) async-start(bf16[288,8,128]{2,0,1:T(8,128)(2,1)} %bitcast.295), calls=%async_computation.1 | async-start | bytes 1179648 | tf_op jit(solution)/shard_map/all_to_all | solution.py:114
  111.1 85.2 %all-to-all-start.2 = ((bf16[288,8,128]{2,0,1:T(8,128)(2,1)}), bf16[288,8,128]{2,0,1:T(8,128)(2,1)S(1)}, u32[]{:S(2)}, u32[]{:S(2)}) async-start(bf16[288,8,128]{2,0,1:T(8,128)(2,1)} %bitcast.294), calls=%async_computation.2 | async-start | bytes 1179648 | tf_op jit(solution)/shard_map/all_to_all | solution.py:115
  196.3 4.3 copy-start.22
  196.3 82.0 %all-to-all-start = ((bf16[288,16,128]{2,0,1:T(8,128)(2,1)}), bf16[288,16,128]{2,0,1:T(8,128)(2,1)}, u32[]{:S(2)}, u32[]{:S(2)}) async-start(bf16[288,16,128]{2,0,1:T(8,128)(2,1)} %bitcast.290), calls=%async_computation | async-start | bytes 2359296 | tf_op jit(solution)/shard_map/all_to_all | solution.py:113
  277.1 5.8 copy-start.16
  278.3 20.3 all-to-all-start.3
  306.2 32.7 %copy-start.3 = (f32[4,288,4,128]{3,1,0,2:T(8,128)S(1)}, f32[4,288,4,128]{3,1,0,2:T(8,128)}, u32[]{:S(2)}) copy-start(f32[4,288,4,128]{3,1,0,2:T(8,128)} %copy.152) | copy-start | bytes 7077892
  341.0 10.3 copy-start.49
  347.8 18.4 all-to-all-start.4
  374.2 689.9 %copy-start.10 = (f32[288,2048]{1,0:T(8,128)}, f32[288,2048]{1,0:T(8,128)S(1)}, u32[]{:S(2)}) copy-start(f32[288,2048]{1,0:T(8,128)S(1)} %get-tuple-element.258) | copy-start | bytes 7077892
  375.1 197.8 %copy-start.26 = (bf16[288,2048]{1,0:T(8,128)(2,1)}, bf16[288,2048]{1,0:T(8,128)(2,1)S(1)}, u32[]{:S(2)}) copy-start(bf16[288,2048]{1,0:T(8,128)(2,1)S(1)} %multiply_convert_fusion.4) | copy-start | bytes 3538948
  589.2 423.0 %copy-start.24 = (bf16[1,288,2048]{2,1,0:T(8,128)(2,1)S(1)}, bf16[1,288,2048]{2,1,0:T(8,128)(2,1)}, u32[]{:S(2)}) copy-start(bf16[1,288,2048]{2,1,0:T(8,128)(2,1)} %param.21) | copy-start | bytes 3538948
  1066.4 7.0 copy-start.12
  1074.6 19.2 all-to-all-start.5
  1078.2 307.8 %reduce-scatter.12.cloned.1.call-start = ((), (), s32[]{:S(2)}) async-start(), calls=%async_computation.26 | async-start | bytes 4718592 | tf_op jit(solution)/shard_map/reduce_scatter | solution.py:276
  1219.0 12.7 copy-start.7
  1219.0 12.7 copy-start.41
  1219.0 12.7 copy-start.43
  1231.7 4.5 copy-start.36
  1236.3 149.8 %reduce-scatter.14.cloned.1.call-start = ((), (), s32[]{:S(2)}) async-start(), calls=%async_computation.27 | async-start | bytes 4718592 | tf_op jit(solution)/shard_map/reduce_scatter | solution.py:279
  1253.7 170.6 %reduce-scatter.18.cloned.1.call-start = ((), (), s32[]{:S(2)}) async-start(), calls=%async_computation.29 | async-start | bytes 9437184 | tf_op jit(solution)/shard_map/reduce_scatter | solution.py:285
  1263.6 251.0 %reduce-scatter.10.cloned.1.call-start = ((), (), s32[]{:S(2)}) async-start(), calls=%async_computation.25 | async-start | bytes 9437184 | tf_op jit(solution)/shard_map/reduce_scatter | solution.py:273
  1290.5 6.9 copy-start.28
  1297.5 307.4 %reduce-scatter.16.cloned.1.call-start = ((), (), s32[]{:S(2)}) async-start(), calls=%async_computation.28 | async-start | bytes 9437184 | tf_op jit(solution)/shard_map/reduce_scatter | solution.py:282
  1323.9 7.0 copy-start.30
  1331.0 521.7 %reduce-scatter.20.cloned.1.call-start = ((), (), s32[]{:S(2)}) async-start(), calls=%async_computation.30 | async-start | bytes 28311552 | tf_op jit(solution)/shard_map/reduce_scatter | solution.py:193
  1350.9 985.5 %reduce-scatter.22.cloned.1.call-start = ((), (), s32[]{:S(2)}) async-start(), calls=%async_computation.31 | async-start | bytes 56623104
  1385.9 1210.4 %all-reduce.8.cloned.1.call-start = ((), (), s32[]{:S(2)}) async-start(), calls=%async_computation.32 | async-start | bytes 27262976 | tf_op jit(solution)/shard_map/psum | solution.py:308
  2338.3 15.3 copy-start.29
  2353.6 5.3 copy-start.37
  2353.6 5.3 copy-start.46
  2360.3 5.5 copy-start.19
  2360.3 5.5 copy-start.20
  2596.3 9.4 copy-start.21
  2605.8 3.6 copy-start.34
  (27 other events, 45.3 us)
Sparse Core Ops, SparseCore 0:
  9.6 49.5 all-gather.12
  60.8 45.6 all-gather.14
  108.1 80.8 all-gather.10
  190.5 80.5 all-gather.16
  272.5 80.5 all-gather.18
  354.5 218.3 all-gather.20
  574.5 218.0 all-gather.22
  794.2 218.0 all-gather.24
  1236.4 46.4 reduce-scatter.11
  1285.6 48.3 reduce-scatter.13
  1336.3 87.9 reduce-scatter.17
  1426.5 87.9 reduce-scatter.9
  1516.8 87.9 reduce-scatter.15
  1607.1 245.5 reduce-scatter.19
  1854.9 481.4 reduce-scatter.21
  2341.0 255.2 all-reduce.7
where the time goes:
time: 2630 us; the launch traced here: 2620 us
  waiting for transfers between devices  2000 us (76%)
  matrix products  350 us (13%)
  blocking collectives  99.9 us (4%)
  local copies, waits for them, and re-layouts  66.6 us (3%)
  other arithmetic  60.9 us (2%)
    unnamed x17, waiting for transfers between devices  489 us
    reduce_scatter x1, waiting for transfers between devices, shards(): lax.psum_scatter(dot_rows(hidden, grad_out).astype(jnp.bfloat16), 'fsdp',...  248 us
    all_gather x1, waiting for transfers between devices, shards(): lax.all_gather(w_down, 'fsdp', axis=0, tiled=True)  204 us
    all_gather x1, waiting for transfers between devices, shards(): lax.all_gather(w_up, 'fsdp', axis=0, tiled=True)  203 us
    all_gather x1, waiting for transfers between devices, shards(): lax.all_gather(w_gate, 'fsdp', axis=0, tiled=True)  198 us
    psum x1, waiting for transfers between devices, shards(): lax.psum(part_query.astype(jnp.bfloat16), 'seq').astype(jnp.float32)  194 us
    reduce_scatter x1, waiting for transfers between devices, shards(): lax.psum_scatter(grad_w_attn_gate.astype(jnp.bfloat16), 'fsdp', scatter_d...  90.3 us
    reduce_scatter x1, waiting for transfers between devices, shards(): lax.psum_scatter(grad_w_query.astype(jnp.bfloat16), 'fsdp', scatter_dimen...  90.2 us
  transfers between devices with their start and end apart: 22, of which 16 were waited for; matrix products, arithmetic and copies ran while one was open for 10% of the time, Pallas kernels for 0%

commit v1 on v0

--- a/solution.py
+++ b/solution.py
@@ -10,6 +10,18 @@
 epsilon = 1e-06
 rope_base = 1000000.0
 masked_value = -1e30
+
+
+def doubled_up(array, axis, dim):
+    ways, here, step = (lax.axis_size(axis), lax.axis_index(axis), array.shape[dim])
+    line, have = (array, 1)
+    while have < ways:
+        line = jnp.concatenate(
+            [line, lax.ppermute(line, axis, [(d, (d - have) % ways) for d in range(ways)])],
+            axis=dim,
+        )
+        have = 2 * have
+    return jnp.roll(line, here * step, axis=dim)
 
 
 def dot_plain(left_mat, right_mat):
@@ -83,7 +95,7 @@
         lax.all_gather(w_query, "fsdp", axis=0, tiled=True),
         lax.all_gather(key_matrix, "fsdp", axis=0, tiled=True),
         lax.all_gather(value_matrix, "fsdp", axis=0, tiled=True),
-        lax.all_gather(w_attn_gate, "fsdp", axis=0, tiled=True),
+        doubled_up(w_attn_gate, "fsdp", 0),
         lax.all_gather(w_out, "fsdp", axis=0, tiled=True),
         lax.all_gather(gain_attn, "fsdp", axis=0, tiled=True),
         lax.all_gather(gain_mlp, "fsdp", axis=0, tiled=True),

time: 2630 us -> 2750 us (1.046)
  blocking collectives: 99.9 us -> 237 us
  waiting for transfers between devices: 2000 us -> 1940 us
    ppermute x0 -> x3, waiting for transfers between devices: none -> 267 us  [doubled_up(): lax.ppermute(line, axis, [(d, (d - have) % ways) for d in range(ways)])]
    all_gather x1, waiting for transfers between devices: 198 us -> 88.6 us  [shards(): lax.all_gather(w_gate, 'fsdp', axis=0, tiled=True)]
    all_gather x1, blocking collectives: 13.6 us -> 115 us  [shards(): lax.all_gather(gain_attn, 'fsdp', axis=0, tiled=True)]
    all_gather x1, waiting for transfers between devices: 74.3 us -> 0.02 us  [shards(): lax.all_gather(w_query, 'fsdp', axis=0, tiled=True)]
    all_gather x1 -> x0, waiting for transfers between devices: 69.2 us -> none  [shards(): lax.all_gather(w_attn_gate, 'fsdp', axis=0, tiled=True)]
    all_gather x1, waiting for transfers between devices: 39.1 us -> 0.01 us  [shards(): lax.all_gather(value_matrix, 'fsdp', axis=0, tiled=True)]
    all_gather x1, blocking collectives: 8.98 us -> 42.4 us  [shards(): lax.all_gather(gain_mlp, 'fsdp', axis=0, tiled=True)]
    unnamed x17 -> x16, waiting for transfers between devices: 489 us -> 488 us
  transfers between devices with their start and end apart: 22 -> 24, of which waited for: 16 -> 16; matrix products, arithmetic and copies ran while one was open for 10% -> 10% of each run, Pallas kernels for 0% -> 0%
where the time goes in v1:
time: 2750 us; the launch traced here: 2740 us
  waiting for transfers between devices  1940 us (71%)
  matrix products  356 us (13%)
  blocking collectives  237 us (9%)
  local copies, waits for them, and re-layouts  90 us (3%)
  other arithmetic  61 us (2%)
  starting transfers between devices  31.5 us (1%)
    unnamed x16, waiting for transfers between devices  488 us
    ppermute x3, waiting for transfers between devices, doubled_up(): lax.ppermute(line, axis, [(d, (d - have) % ways) for d in range(ways)])  267 us
    reduce_scatter x1, waiting for transfers between devices, shards(): lax.psum_scatter(dot_rows(hidden, grad_out).astype(jnp.bfloat16), 'fsdp',...  248 us
    all_gather x1, waiting for transfers between devices, shards(): lax.all_gather(w_down, 'fsdp', axis=0, tiled=True)  204 us
    all_gather x1, waiting for transfers between devices, shards(): lax.all_gather(w_up, 'fsdp', axis=0, tiled=True)  203 us
    psum x1, waiting for transfers between devices, shards(): lax.psum(part_query.astype(jnp.bfloat16), 'seq').astype(jnp.float32)  190 us
    all_gather x1, blocking collectives, shards(): lax.all_gather(gain_attn, 'fsdp', axis=0, tiled=True)  115 us
    reduce_scatter x1, waiting for transfers between devices, shards(): lax.psum_scatter(grad_w_attn_gate.astype(jnp.bfloat16), 'fsdp', scatter_d...  90.3 us
  transfers between devices with their start and end apart: 24, of which 16 were waited for; matrix products, arithmetic and copies ran while one was open for 10% of the time, Pallas kernels for 0%

profile of v1, /device:TPU:0, one launch (start us, length us, event | category | flops | bytes accessed | tf_op | source)
XLA Modules:
  0.0 2739.5 jit_solution(18174893354743430318)
XLA Ops:
  16.5 28.7 %collective-permute-done = bf16[256,2048]{1,0:T(8,128)(2,1)S(1)} collective-permute-done((bf16[256,2048]{1,0:T(8,128)(2,1)S(1)}, bf16[256,2048]{1,0:T(8,128)(2,1)S(1)}, u32[]{:S(2)}, u32[]{:S(2)}) %collective-permute-start) | collective-permute-done | bytes 1048608 | tf_op jit(solution)/shard_map/ppermute | solution.py:20
  45.5 60.9 %collective-permute-done.1 = bf16[512,2048]{1,0:T(8,128)(2,1)S(1)} collective-permute-done((bf16[512,2048]{1,0:T(8,128)(2,1)S(1)}, bf16[512,2048]{1,0:T(8,128)(2,1)S(1)}, u32[]{:S(2)}, u32[]{:S(2)}) %collective-permute-start.1) | collective-permute-done | bytes 2097184 | tf_op jit(solution)/shard_map/ppermute | solution.py:20
  111.2 115.3 %all-gather = bf16[8,1,256]{2,1,0:T(2,128)(2,1)S(1)} all-gather(bf16[1,1,256]{2,1,0:T(2,128)(2,1)S(1)} %reshape.498), channel_id=1, replica_groups=mesh['seq'=4,'fsdp'=8] {'fsdp'}, dimensions={0}, use_global_device_ids=true | all-gather | bytes 4608 | tf_op jit(solution)/shard_map/all_gather | solution.py:100
  246.8 177.1 %collective-permute-done.2 = bf16[1024,2048]{1,0:T(8,128)(2,1)} collective-permute-done((bf16[1024,2048]{1,0:T(8,128)(2,1)}, bf16[1024,2048]{1,0:T(8,128)(2,1)}, u32[]{:S(2)}, u32[]{:S(2)}) %collective-permute-start.2) | collective-permute-done | bytes 4194336 | tf_op jit(solution)/shard_map/ppermute | solution.py:20
  446.7 6.1 fusion.91
  461.8 6.5 fusion.94
  469.5 5.9 all-to-all-done.3
  483.1 11.5 all-to-all-done
  501.3 32.6 %while.28 = (s32[]{:T(128)}, f32[2,576,2,2,128]{4,1,0,3,2:T(8,128)}, f32[2,2,2,576]{3,2,1,0:T(2,128)}, s32[2]{0:T(128)S(1)}, s32[1152]{0:T(1024)S(1)}, /*index=5...) while((s32[]{:T(128)}, ...), condition=%wide.region_6.7_spmd.clone, body=%wide.region_3.6_spmd.clone.sunk | while | flops 1392793856 | bytes 37545896 | solution.py:175
  536.1 6.7 copy.153
  546.4 42.4 %all-gather.1 = bf16[8,1,256]{2,1,0:T(2,128)(2,1)S(1)} all-gather(bf16[1,1,256]{2,1,0:T(2,128)(2,1)S(1)} %reshape.500), channel_id=1, replica_groups=mesh['seq'=4,'fsdp'=8] {'fsdp'}, dimensions={0}, use_global_device_ids=true | all-gather | bytes 4608 | tf_op jit(solution)/shard_map/all_gather | solution.py:101
  597.5 88.6 %all-gather.18.cloned.1.call-done = bf16[2048,6144]{1,0:T(8,128)(2,1)} async-done(((bf16[256,6144]{1,0:T(8,128)(2,1)}), bf16[2048,6144]{1,0:T(8,128)(2,1)}) %all-gather.18.cloned.1.call-update) | async-done | bytes 25165840 | tf_op jit(solution)/shard_map/all_gather | solution.py:186
  686.1 16.2 fusion.119
  702.3 203.3 %all-gather.20.cloned.1.call-done = bf16[2048,6144]{1,0:T(8,128)(2,1)} async-done(((bf16[256,6144]{1,0:T(8,128)(2,1)}), bf16[2048,6144]{1,0:T(8,128)(2,1)}) %all-gather.20.cloned.1.call-update) | async-done | bytes 25165840 | tf_op jit(solution)/shard_map/all_gather | solution.py:187
  905.6 15.3 fusion.120
  920.8 204.4 %all-gather.22.cloned.1.call-done = bf16[6144,2048]{1,0:T(8,128)(2,1)} async-done(((bf16[768,2048]{1,0:T(8,128)(2,1)}), bf16[6144,2048]{1,0:T(8,128)(2,1)}) %all-gather.22.cloned.1.call-update) | async-done | bytes 25165840 | tf_op jit(solution)/shard_map/all_gather | solution.py:188
  1125.3 20.9 multiply_convert_fusion
  1146.2 14.5 fusion.121
  1160.7 15.7 multiply_reduce_fusion
  1179.4 6.9 fusion.95
  1191.2 15.6 all-to-all-done.5
  1209.6 115.0 %while.29 = (s32[]{:T(128)}, f32[1152,2,128]{0,2,1:T(8,128)}, f32[1152,2,128]{0,2,1:T(8,128)S(1)}, f32[2,576,2,2,128]{4,1,0,3,2:T(8,128)}, s32[2]{0:T(128)S(1)},...) while((s32[]{:T(128)}, f32[1152,2,128]{0,2,1:T(8,128)}, ...), condition=%wide.region_11.12_spmd.clone, body=%wide.region_9.11_spmd.clone.sunk | while | flops 3437723136 | bytes 128183776 | solution.py:254
  1214.5 7.9 fusion.188
  1228.0 16.5 fusion.192
  1244.4 17.2 fusion.190
  1271.8 7.9 fusion.188
  1285.3 16.4 fusion.192
  1301.7 17.5 fusion.190
  1331.0 11.6 all_to_all.129
  1354.4 11.2 all_to_all.130
  1373.7 8.1 convolution_convert_fusion.2
  1392.6 15.5 all_to_all.131
  1410.2 8.2 convolution_convert_fusion.3
  1427.1 14.5 all_to_all.132
  1443.0 6.9 convolution_convert_fusion.4
  1451.2 18.6 convolution_convert_fusion.1
  1471.2 33.7 %convolution_convert_fusion = bf16[2048,12288]{1,0:T(8,128)(2,1)} fusion(bf16[288,2048]{1,0:T(8,128)(2,1)S(1)} %copy-done.34, bf16[288,6144]{1,0:T(8,128)(2,1)} %get-tuple-element.240, bf16[288,6144]{1,0:T(8,128)(2,1)} %get-tuple-element.241), kind=kOutput, calls=%fused_computation.61 | convolution fusion | flops 14534836224 | bytes 58589184 | tf_op jit(solution)/shard_map/dot_general | solution.py:32
  1505.2 35.3 %reduce-scatter.18.cloned.1.call-done = bf16[256,2048]{1,0:T(8,128)(2,1)} async-done(((bf16[2048,2048]{1,0:T(8,128)(2,1)}), bf16[256,2048]{1,0:T(8,128)(2,1)}) %reduce-scatter.18.cloned.1.call-update) | async-done | bytes 1048592 | tf_op jit(solution)/shard_map/reduce_scatter | solution.py:297
  1540.5 90.3 %reduce-scatter.16.cloned.1.call-done = bf16[256,2048]{1,0:T(8,128)(2,1)} async-done(((bf16[2048,2048]{1,0:T(8,128)(2,1)}), bf16[256,2048]{1,0:T(8,128)(2,1)}) %reduce-scatter.16.cloned.1.call-update) | async-done | bytes 1048592 | tf_op jit(solution)/shard_map/reduce_scatter | solution.py:294
  1630.9 90.2 %reduce-scatter.10.cloned.1.call-done = bf16[256,2048]{1,0:T(8,128)(2,1)} async-done(((bf16[2048,2048]{1,0:T(8,128)(2,1)}), bf16[256,2048]{1,0:T(8,128)(2,1)}) %reduce-scatter.10.cloned.1.call-update) | async-done | bytes 1048592 | tf_op jit(solution)/shard_map/reduce_scatter | solution.py:285
  1721.0 247.9 %reduce-scatter.20.cloned.1.call-done = bf16[768,2048]{1,0:T(8,128)(2,1)} async-done(((bf16[6144,2048]{1,0:T(8,128)(2,1)}), bf16[768,2048]{1,0:T(8,128)(2,1)}) %reduce-scatter.20.cloned.1.call-update) | async-done | bytes 3145744 | tf_op jit(solution)/shard_map/reduce_scatter | solution.py:205
  1969.0 483.8 %reduce-scatter.22.cloned.1.call-done = bf16[256,12288]{1,0:T(8,128)(2,1)} async-done(((bf16[2048,12288]{1,0:T(8,128)(2,1)}), bf16[256,12288]{1,0:T(8,128)(2,1)}) %reduce-scatter.22.cloned.1.call-update) | async-done | bytes 6291472
  2454.6 15.0 fusion.76
  2478.9 8.7 fusion.83
  2487.5 14.6 all-reduce.3
  2504.2 11.5 all-reduce.4
  2522.3 190.4 %all-reduce.8.cloned.1.call-done = (bf16[256,2048]{1,0:T(8,128)(2,1)}, bf16[256,1024]{1,0:T(8,128)(2,1)}, bf16[256,1024]{1,0:T(8,128)(2,1)}, bf16[256,2048]{1,0:...) async-done(((bf16[256,2048]{1,0:T(8,128)(2,1)}, bf16[256,1024]{1,0:T(8,128)(2,1)}, bf16[256,1024]{1,0:T(8,128)(2,1)}, ...) | async-done | bytes 13631504 | tf_op jit(solution)/shard_map/psum | solution.py:320
  2712.7 9.4 fusion.118
  (296 shorter events, 244.1 us)
Async XLA Ops:
  7.2 230.5 %all-gather.12.cloned.1.call-start = ((), (), s32[]{:S(2)}) async-start(), calls=%async_computation.18 | async-start | bytes 4718592 | tf_op jit(solution)/shard_map/all_gather | solution.py:96
  7.9 423.4 %all-gather.14.cloned.1.call-start = ((), (), s32[]{:S(2)}) async-start(), calls=%async_computation.19 | async-start | bytes 4718592 | tf_op jit(solution)/shard_map/all_gather | solution.py:97
  8.7 453.1 %all-gather.10.cloned.1.call-start = ((), (), s32[]{:S(2)}) async-start(), calls=%async_computation.17 | async-start | bytes 9437184 | tf_op jit(solution)/shard_map/all_gather | solution.py:95
  9.4 581.5 %all-gather.16.cloned.1.call-start = ((), (), s32[]{:S(2)}) async-start(), calls=%async_computation.20 | async-start | bytes 9437184 | tf_op jit(solution)/shard_map/all_gather | solution.py:99
  10.0 676.1 %all-gather.18.cloned.1.call-start = ((), (), s32[]{:S(2)}) async-start(), calls=%async_computation.21 | async-start | bytes 28311552 | tf_op jit(solution)/shard_map/all_gather | solution.py:186
  10.6 895.0 %all-gather.20.cloned.1.call-start = ((), (), s32[]{:S(2)}) async-start(), calls=%async_computation.22 | async-start | bytes 28311552 | tf_op jit(solution)/shard_map/all_gather | solution.py:187
  11.1 1114.1 %all-gather.22.cloned.1.call-start = ((), (), s32[]{:S(2)}) async-start(), calls=%async_computation.23 | async-start | bytes 28311552 | tf_op jit(solution)/shard_map/all_gather | solution.py:188
  11.9 33.3 %collective-permute-start = (bf16[256,2048]{1,0:T(8,128)(2,1)S(1)}, bf16[256,2048]{1,0:T(8,128)(2,1)S(1)}, u32[]{:S(2)}, u32[]{:S(2)}) collective-permute-start(bf16[256,2048]{1,0:T(8,128)(2,1)S(1)} %copy-done.5), channel_id=1, source_target_pairs={{0,7},{1,0},{2,1},{3,2},{4,3},{5,4},{6,5},{7,6},{8,15},{9,8},{10,9... | collective-permute-start | bytes 3145736 | tf_op jit(solution)/shard_map/ppermute | solution.py:20
  45.2 63.5 %copy-start.6 = (bf16[256,2048]{1,0:T(8,128)(2,1)}, bf16[256,2048]{1,0:T(8,128)(2,1)S(1)}, u32[]{:S(2)}) copy-start(bf16[256,2048]{1,0:T(8,128)(2,1)S(1)} %collective-permute-done) | copy-start | bytes 3145732
  45.4 65.8 %copy-start.56 = (bf16[256]{0:T(256)(128)(2,1)S(1)}, bf16[256]{0:T(256)(128)(2,1)}, u32[]{:S(2)}) copy-start(bf16[256]{0:T(256)(128)(2,1)} %param.30) | copy-start | bytes 1540
  45.4 181.1 %copy-start.57 = (s32[1,4]{1,0:T(1,128)S(1)}, s32[1,4]{1,0:T(1,128)}, u32[]{:S(2)}) copy-start(s32[1,4]{1,0:T(1,128)} %param.19) | copy-start | bytes 52
  45.4 181.3 %copy-start.52 = (s32[1,1152]{1,0:T(1,128)S(1)}, s32[1,1152]{1,0:T(1,128)}, u32[]{:S(2)}) copy-start(s32[1,1152]{1,0:T(1,128)} %param.20) | copy-start | bytes 13828
  45.4 61.0 %collective-permute-start.1 = (bf16[512,2048]{1,0:T(8,128)(2,1)S(1)}, bf16[512,2048]{1,0:T(8,128)(2,1)S(1)}, u32[]{:S(2)}, u32[]{:S(2)}) collective-permute-start(bf16[512,2048]{1,0:T(8,128)(2,1)S(1)} %pad_maximum_fusion.1), channel_id=1, source_target_pairs={{0,6},{1,7},{2,0},{3,1},{4,2},{5,3},{6,4},{7,5},{8,14},{9,15},{10,... | collective-permute-start | bytes 6291464 | tf_op jit(solution)/shard_map/ppermute | solution.py:20
  108.7 315.2 %collective-permute-start.2 = (bf16[1024,2048]{1,0:T(8,128)(2,1)}, bf16[1024,2048]{1,0:T(8,128)(2,1)}, u32[]{:S(2)}, u32[]{:S(2)}) collective-permute-start(bf16[1024,2048]{1,0:T(8,128)(2,1)} %pad_maximum_fusion), channel_id=1, source_target_pairs={{0,4},{1,5},{2,6},{3,7},{4,0},{5,1},{6,2},{7,3},{8,12},{9,13},{10,... | collective-permute-start | bytes 12582920 | tf_op jit(solution)/shard_map/ppermute | solution.py:20
  226.5 235.3 %copy-start.47 = (f32[8,1,256]{2,1,0:T(1,128)}, f32[8,1,256]{2,1,0:T(1,128)S(1)}, u32[]{:S(2)}) copy-start(f32[8,1,256]{2,1,0:T(1,128)S(1)} %convert_element_type.307) | copy-start | bytes 24580
  228.5 233.3 %copy-start.50 = (f32[288]{0:T(512)}, f32[288]{0:T(512)S(1)}, u32[]{:S(2)}) copy-start(f32[288]{0:T(512)S(1)} %add_rsqrt_fusion.1) | copy-start | bytes 3460
  242.6 200.1 %all-to-all-start.1 = ((bf16[288,8,128]{2,0,1:T(8,128)(2,1)}), bf16[288,8,128]{2,0,1:T(8,128)(2,1)}, u32[]{:S(2)}, u32[]{:S(2)}) async-start(bf16[288,8,128]{2,0,1:T(8,128)(2,1)} %bitcast.354), calls=%async_computation.1 | async-start | bytes 1179648 | tf_op jit(solution)/shard_map/all_to_all | solution.py:126
  437.8 8.9 copy-start.23
  442.7 13.5 all-to-all-start.2
  456.9 18.5 all-to-all-start.3
  468.3 11.7 copy-start.20
  468.3 11.7 copy-start.21
  475.4 19.2 all-to-all-start
  483.1 50.8 %copy-start.3 = (f32[4,288,4,128]{3,1,0,2:T(8,128)}, f32[4,288,4,128]{3,1,0,2:T(8,128)S(1)}, u32[]{:S(2)}) copy-start(f32[4,288,4,128]{3,1,0,2:T(8,128)S(1)} %copy.152) | copy-start | bytes 7077892
  536.1 10.3 copy-start.58
  542.8 46.0 %all-to-all-start.4 = ((bf16[1152,4,128]{2,1,0:T(4,128)(2,1)}), bf16[1152,4,128]{2,1,0:T(4,128)(2,1)S(1)}, u32[]{:S(2)}, u32[]{:S(2)}) async-start(bf16[1152,4,128]{2,1,0:T(4,128)(2,1)} %copy.153), calls=%async_computation.4 | async-start | bytes 2359296 | tf_op jit(solution)/shard_map/all_to_all | solution.py:179
  596.6 580.5 %copy-start.13 = (f32[288,2048]{1,0:T(8,128)}, f32[288,2048]{1,0:T(8,128)S(1)}, u32[]{:S(2)}) copy-start(f32[288,2048]{1,0:T(8,128)S(1)} %get-tuple-element.258) | copy-start | bytes 7077892
  597.5 88.6 %copy-start.33 = (bf16[288,2048]{1,0:T(8,128)(2,1)}, bf16[288,2048]{1,0:T(8,128)(2,1)S(1)}, u32[]{:S(2)}) copy-start(bf16[288,2048]{1,0:T(8,128)(2,1)S(1)} %multiply_convert_fusion.4) | copy-start | bytes 3538948
  702.3 423.0 %copy-start.31 = (bf16[1,288,2048]{2,1,0:T(8,128)(2,1)S(1)}, bf16[1,288,2048]{2,1,0:T(8,128)(2,1)}, u32[]{:S(2)}) copy-start(bf16[1,288,2048]{2,1,0:T(8,128)(2,1)} %param.21) | copy-start | bytes 3538948
  1179.4 7.0 copy-start.15
  1186.4 20.5 copy-start.10
  1187.6 19.2 all-to-all-start.5
  1191.2 314.0 %reduce-scatter.12.cloned.1.call-start = ((), (), s32[]{:S(2)}) async-start(), calls=%async_computation.25 | async-start | bytes 4718592 | tf_op jit(solution)/shard_map/reduce_scatter | solution.py:288
  1331.0 15.9 copy-start.25
  1331.0 15.9 copy-start.48
  1331.0 15.9 copy-start.51
  1352.5 152.8 %reduce-scatter.14.cloned.1.call-start = ((), (), s32[]{:S(2)}) async-start(), calls=%async_computation.26 | async-start | bytes 4718592 | tf_op jit(solution)/shard_map/reduce_scatter | solution.py:291
  1372.0 168.5 %reduce-scatter.18.cloned.1.call-start = ((), (), s32[]{:S(2)}) async-start(), calls=%async_computation.28 | async-start | bytes 9437184 | tf_op jit(solution)/shard_map/reduce_scatter | solution.py:297
  1381.8 249.0 %reduce-scatter.16.cloned.1.call-start = ((), (), s32[]{:S(2)}) async-start(), calls=%async_computation.27 | async-start | bytes 9437184 | tf_op jit(solution)/shard_map/reduce_scatter | solution.py:294
  1418.5 302.5 %reduce-scatter.10.cloned.1.call-start = ((), (), s32[]{:S(2)}) async-start(), calls=%async_computation.24 | async-start | bytes 9437184 | tf_op jit(solution)/shard_map/reduce_scatter | solution.py:285
  1443.0 6.9 copy-start.36
  1449.9 519.0 %reduce-scatter.20.cloned.1.call-start = ((), (), s32[]{:S(2)}) async-start(), calls=%async_computation.29 | async-start | bytes 28311552 | tf_op jit(solution)/shard_map/reduce_scatter | solution.py:205
  1469.9 982.8 %reduce-scatter.22.cloned.1.call-start = ((), (), s32[]{:S(2)}) async-start(), calls=%async_computation.30 | async-start | bytes 56623104
  1504.9 1207.8 %all-reduce.8.cloned.1.call-start = ((), (), s32[]{:S(2)}) async-start(), calls=%async_computation.31 | async-start | bytes 27262976 | tf_op jit(solution)/shard_map/psum | solution.py:320
  2454.6 15.0 copy-start.37
  2478.8 8.7 copy-start.53
  2478.9 40.0 %copy-start.17 = (f32[288,2048]{1,0:T(8,128)S(1)}, f32[288,2048]{1,0:T(8,128)}, u32[]{:S(2)}) copy-start(f32[288,2048]{1,0:T(8,128)} %copy-done.15) | copy-start | bytes 7077892
  2712.7 9.4 copy-start.28
  (38 other events, 80.5 us)
Sparse Core Ops, SparseCore 0:
  9.6 67.8 all-gather.11
  79.0 177.7 all-gather.13
  258.5 114.7 all-gather.9
  374.7 89.6 all-gather.15
  465.9 220.0 all-gather.17
  687.6 217.9 all-gather.19
  907.2 218.0 all-gather.21
  1352.6 46.4 reduce-scatter.11
  1401.9 48.3 reduce-scatter.13
  1452.5 88.0 reduce-scatter.17
  1542.8 87.9 reduce-scatter.15
  1633.0 87.9 reduce-scatter.9
  1723.4 245.5 reduce-scatter.19
  1971.2 481.4 reduce-scatter.21
  2457.3 255.2 all-reduce.7
